TPU v7x, 256 devices: a whole 4x4x8 slice. The times are simulated.
256 devices in a mesh: rows: 32 (over z, x), cols: 8 (over y, core).
Axes of the slice: x: 4, y: 4, z: 8, core: 2. Of those that a mesh axis runs over, the one named last changes fastest.
Arguments:
- block_values: bfloat16 [256, 256, 128, 128], P('rows', 'cols')
- block_columns: int32 [256, 256], P('rows', 'cols'), may hold values from 0 to 1023, as said below
- row_counts: int32 [256, 8], P('rows', 'cols'), may hold values from 1 to 32, as said below
- sketch: bfloat16 [1048576, 256], P(('rows', 'cols')), may hold values from -6 to 6
Outputs:
- basis: float32 [32768, 256], P(('rows', 'cols'))
- triangle: float32 [256, 256], replicated
Inputs may be any that keep to these rules, and one draw needn't show every extreme that they name: row_counts[b, c] counts the live slots among slots c * 32 to c * 32 + 31 of block-row b; some entry equals 32. `block_columns`: take the 8 x 32 slots of one index of rows and one column group c; among them at most 12 name block-columns j with the same j // 32, and in every such set some j // 32 is named by exactly 12 slots.
All inputs are finite; a program needn't handle non-finite values.
Results may differ from a plain program's by a relative error of at most 0.0003.
Values may be sent and summed in bfloat16 or wider, within the bound.
No kernel may reach another device: no remote copies, remote signals or barrier semaphores. Data moves between devices by JAX's collectives and lax.ppermute only.
A program may use at most 128 MiB of HBM per device.

v0:
```python
import jax
import jax.numpy as jnp
from jax import lax
from jax.sharding import PartitionSpec as P


def request_table(columns_flat, per_owner, axis_rows, capacity):
    owners = columns_flat // per_owner
    onehot = (owners[:, None] == jnp.arange(axis_rows, dtype=jnp.int32)[None, :]).astype(jnp.int32)
    before = jnp.cumsum(onehot, axis=0) - onehot
    ranking = jnp.sum(before * onehot, axis=1)
    position = owners * capacity + ranking
    wanted = (
        jnp.zeros((axis_rows * capacity,), jnp.int32).at[position].set(columns_flat % per_owner)
    )
    return (position, wanted.reshape(axis_rows, capacity))


def send_back(wanted, local_blocks):
    blocks = local_blocks[wanted]
    return lax.all_to_all(blocks, "rows", split_axis=0, concat_axis=0, tiled=True)


def row_products(values_rows, positions_rows, counts_rows, table):
    slot_count = values_rows.shape[1]
    slot_ids = jnp.arange(slot_count, dtype=jnp.int32)

    def one_row(entries):
        values_row, positions_row, counts_row = entries
        picked = table[positions_row]
        live_mask = (slot_ids < counts_row[0]).astype(jnp.bfloat16)
        picked = picked * live_mask[:, None, None]
        return jnp.einsum("sab,sbk->ak", values_row, picked, preferred_element_type=jnp.float32)

    result = lax.map(one_row, (values_rows, positions_rows, counts_rows))
    return result.reshape(-1, table.shape[2])


def per_device(block_values, block_columns, row_counts, sketch):
    block_order = block_values.shape[2]
    sketch_width = sketch.shape[1]
    axis_rows = lax.axis_size("rows")
    slot_total = block_columns.shape[0] * block_columns.shape[1]
    capacity = 3 * slot_total // (2 * axis_rows)
    local_blocks = sketch.reshape(-1, block_order, sketch_width)
    per_owner = local_blocks.shape[0]
    position, wanted_here = request_table(block_columns.reshape(-1), per_owner, axis_rows, capacity)
    table = send_back(
        lax.all_to_all(wanted_here, "rows", split_axis=0, concat_axis=0, tiled=True), local_blocks
    )
    table = table.reshape(-1, block_order, sketch_width)
    positions = position.reshape(block_columns.shape[0], block_columns.shape[1])
    partial_image = row_products(block_values, positions, row_counts, table)
    image_here = lax.psum_scatter(partial_image, "cols", scatter_dimension=0, tiled=True)
    total_rows = image_here.shape[0] * lax.axis_size("rows") * lax.axis_size("cols")
    gram_local = jnp.dot(
        image_here.T,
        image_here,
        precision=lax.Precision.HIGHEST,
        preferred_element_type=jnp.float32,
    )
    gram_matrix = lax.psum(gram_local, ("rows", "cols")) / total_rows
    lower_factor = jnp.linalg.cholesky(gram_matrix)
    basis_rows = jax.scipy.linalg.solve_triangular(lower_factor, image_here.T, lower=True).T
    return (basis_rows, lower_factor.T)


def solution(mesh):
    return jax.shard_map(
        per_device,
        mesh=mesh,
        in_specs=(
            P("rows", "cols", None, None),
            P("rows", "cols"),
            P("rows", "cols"),
            P(("rows", "cols"), None),
        ),
        out_specs=(P(("rows", "cols"), None), P()),
        check_vma=False,
    )
```

profile of v0, /device:TPU:2, one launch (start us, length us, event | category | flops | bytes accessed | tf_op | source)
XLA Modules:
  0.0 1127.3 jit_solution(16945406172135663035)
XLA Ops:
  7.2 0.9 reshape.225
  8.1 0.8 reshape.224
  8.9 0.8 reshape.228
  10.6 1.4 scatter_custom_fusion
  12.1 20.0 %all_to_all.17 = s32[32,1,12]{2,1,0:T(1,128)S(1)} all-to-all(s32[32,1,12]{2,1,0:T(1,128)S(1)} %bitcast.99), channel_id=1, replica_groups=mesh['rows'=32,'cols'=8] {'rows'}, dimensions={0} | all-to-all | bytes 3072 | tf_op jit(solution)/shard_map/all_to_all | solution.py:49
  32.2 12.9 %gather_fusion.1 = bf16[384,128,256]{2,1,0:T(8,128)(2,1)} fusion(bf16[32,128,256]{2,1,0:T(8,128)(2,1)S(1)} %bitcast.94, s32[1024]{0:T(1024)S(1)} %pad_clamp_fusion.1), kind=kCustom, calls=%fused_computation.1 | custom fusion | bytes 50333184 | tf_op jit(solution)/shard_map/gather | solution.py:20
  45.1 6.5 all-to-all-start.1
  51.7 577.4 %all-to-all-done.1 = bf16[32,12,128,256]{3,2,1,0:T(8,128)(2,1)} async-done(((bf16[32,12,128,256]{3,2,1,0:T(8,128)(2,1)}), bf16[32,12,128,256]{3,2,1,0:T(8,128)(2,1)}, u32[]{:S(2)}, u32[]{:S(2)}) %all-to-all-start.1) | async-done | bytes 25165856 | tf_op jit(solution)/shard_map/all_to_all | solution.py:21
  629.1 95.0 %while.13 = (s32[]{:T(128)}, f32[8,128,256]{2,1,0:T(8,128)S(1)}, bf16[8,32,128,128]{3,2,1,0:T(8,128)(2,1)}, s32[8,32]{1,0:T(8,128)S(1)}, bf16[384,128,256]{2,1,0:T(8,128)(2,1)}, /*index=5*/s32[8,1]{0,1:T(1,128)S(1)}, s32[]{:T(128)}) while((s32[]{:T(128)}, f32[8,128,256]{2,1,0:T(8,128)S(1)}, bf16[8,32,128,128]{3,2,1,0:T(8,128)(2,1)}, ...), condition=%wide.region_5.6_spmd.clone, body=%wide.region_4.5_spmd.clone.sunk | while | flops 269485216 | bytes 7477409 | solution.py:35
  629.1 8.8 gather_fusion
  638.6 0.6 compare_convert_fusion.2
  639.2 1.8 fusion.53
  641.0 8.8 gather_fusion
  650.4 0.6 compare_convert_fusion.2
  651.1 1.8 fusion.53
  652.9 8.8 gather_fusion
  662.3 0.6 compare_convert_fusion.2
  663.0 1.8 fusion.53
  664.8 8.8 gather_fusion
  674.2 0.6 compare_convert_fusion.2
  674.8 1.8 fusion.53
  676.6 8.8 gather_fusion
  686.1 0.6 compare_convert_fusion.2
  686.7 1.8 fusion.53
  688.5 8.8 gather_fusion
  698.6 1.8 fusion.53
  700.4 8.8 gather_fusion
  709.9 0.6 compare_convert_fusion.2
  710.5 1.8 fusion.53
  712.3 8.8 gather_fusion
  721.7 0.6 compare_convert_fusion.2
  722.4 1.8 fusion.53
  724.1 1.3 copy.23
  725.7 70.9 %reduce-scatter.2.cloned.1.call-done = f32[128,256]{0,1:T(8,128)} async-done(((f32[1024,256]{0,1:T(8,128)}), f32[128,256]{0,1:T(8,128)}) %reduce-scatter.2.cloned.1.call-update) | async-done | bytes 131088 | tf_op jit(solution)/shard_map/reduce_scatter | solution.py:54
  796.6 2.1 fusion.37
  798.7 257.2 %all-reduce.3.cloned.1.call-done = f32[256,256]{0,1:T(8,128)} async-done(((f32[256,256]{0,1:T(8,128)}), f32[256,256]{0,1:T(8,128)}) %all-reduce.3.cloned.1.call-update) | async-done | bytes 262160 | tf_op jit(solution)/shard_map/psum | solution.py:62
  1055.9 1.0 broadcast_multiply_fusion
  1057.0 1.0 fusion.16
  1058.0 11.7 %cholesky.50 = f32[128,128]{1,0:T(8,128)S(1)} custom-call(f32[128,128]{1,0:T(8,128)S(1)} %cholesky.118), custom_call_target="Cholesky" | custom-call | tf_op jit(solution)/shard_map/jit(cholesky)/cholesky | solution.py:63
  1069.8 9.8 custom-call.15
  1080.1 11.7 %cholesky.105 = f32[128,128]{1,0:T(8,128)S(1)} custom-call(f32[128,128]{1,0:T(8,128)S(1)} %convolution_subtract_fusion.1), custom_call_target="Cholesky" | custom-call | tf_op jit(solution)/shard_map/jit(cholesky)/cholesky | solution.py:63
  1091.9 0.7 compare_reduce_fusion
  1094.0 4.3 while.12
  1094.8 1.4 bitcast_dynamic-update-slice_fusion.2
  1096.9 1.4 bitcast_dynamic-update-slice_fusion.2
  1098.3 19.7 %custom-call.16 = f32[2,128,128]{1,2,0:T(8,128)S(1)} custom-call(f32[2,128,128]{2,1,0:T(8,128)S(1)} %get-tuple-element.47), custom_call_target="InvertDiagBlocksLowerTriangular" | custom-call | tf_op jit(solution)/shard_map/jit(_solve_triangular)/triangular_solve | solution.py:64
  1118.8 0.8 copy.20
  1119.6 0.8 copy.21
  (74 shorter events, 9.9 us)
Async XLA Ops:
  7.2 25.0 %copy-start = (bf16[4096,256]{1,0:T(8,128)(2,1)S(1)}, bf16[4096,256]{1,0:T(8,128)(2,1)}, u32[]{:S(2)}) copy-start(bf16[4096,256]{1,0:T(8,128)(2,1)} %param.9) | copy-start | bytes 6291460
  45.1 6.6 copy-start.3
  45.1 584.0 %copy-start.4 = (s32[8,1]{0,1:T(1,128)S(1)}, s32[8,1]{0,1:T(1,128)}, u32[]{:S(2)}) copy-start(s32[8,1]{0,1:T(1,128)} %param.8) | copy-start | bytes 100
  45.1 584.0 %all-to-all-start.1 = ((bf16[32,12,128,256]{3,2,1,0:T(8,128)(2,1)}), bf16[32,12,128,256]{3,2,1,0:T(8,128)(2,1)}, u32[]{:S(2)}, u32[]{:S(2)}) async-start(bf16[32,12,128,256]{3,2,1,0:T(8,128)(2,1)} %bitcast.95), calls=%async_computation.1 | async-start | bytes 50331648 | tf_op jit(solution)/shard_map/all_to_all | solution.py:21
  51.6 745.0 %reduce-scatter.2.cloned.1.call-start = ((), (), s32[]{:S(2)}) async-start(), calls=%async_computation.3 | async-start | bytes 1179648 | tf_op jit(solution)/shard_map/reduce_scatter | solution.py:54
  725.5 330.4 %all-reduce.3.cloned.1.call-start = ((), (), s32[]{:S(2)}) async-start(), calls=%async_computation.4 | async-start | bytes 524288 | tf_op jit(solution)/shard_map/psum | solution.py:62
  1056.9 61.1 %copy-start.2 = (f32[128,256]{0,1:T(8,128)S(1)}, f32[128,256]{0,1:T(8,128)}, u32[]{:S(2)}) copy-start(f32[128,256]{0,1:T(8,128)} %reduce-scatter.2.cloned.1.call-done) | copy-start | bytes 393220
  1069.8 50.6 %copy-start.1 = (bf16[4096,256]{1,0:T(8,128)(2,1)S(1)}, bf16[4096,256]{1,0:T(8,128)(2,1)}, u32[]{:S(2)}) copy-start(bf16[4096,256]{1,0:T(8,128)(2,1)} %param.9) | copy-start | bytes 6291460
Sparse Core Ops, SparseCore 0:
  725.6 70.9 reduce-scatter.1
  802.6 253.2 all-reduce.2
where the time goes:
time: 1130 us
  waiting for transfers between devices  905 us (80%)
  local copies, waits for them, and re-layouts  99.9 us (9%)
  other arithmetic  61.6 us (5%)
  blocking collectives  20 us (2%)
  matrix products  17.3 us (2%)
  between operations  15.6 us (1%)
    all_to_all x1, waiting for transfers between devices, send_back(): lax.all_to_all(blocks, 'rows', split_axis=0, concat_axis=0, tiled=True)  577 us
    psum x1, waiting for transfers between devices, per_device(): gram_matrix = lax.psum(gram_local, ('rows', 'cols')) / total_rows  257 us
    reduce_scatter x1, waiting for transfers between devices, per_device(): lax.psum_scatter(partial_image, 'cols', scatter_dimension=0, tiled=True)  70.9 us
    gather x8, local copies, waits for them, and re-layouts, one_row(): picked = table[positions_row]  70.7 us
    another operation x6, other arithmetic, per_device(): lower_factor = jnp.linalg.cholesky(gram_matrix)  34 us
  transfers between devices with their start and end apart: 3, of which 3 were waited for; matrix products, arithmetic and copies ran while one was open for 0% of the time, Pallas kernels for 0%

commit v1 on v0

--- a/solution.py
+++ b/solution.py
@@ -59,7 +59,7 @@
         precision=lax.Precision.HIGHEST,
         preferred_element_type=jnp.float32,
     )
-    gram_matrix = lax.psum(gram_local, ("rows", "cols")) / total_rows
+    gram_matrix = lax.psum(lax.psum(gram_local, "rows"), "cols") / total_rows
     lower_factor = jnp.linalg.cholesky(gram_matrix)
     basis_rows = jax.scipy.linalg.solve_triangular(lower_factor, image_here.T, lower=True).T
     return (basis_rows, lower_factor.T)

time: 1130 us -> 1080 us (0.956)
  waiting for transfers between devices: 905 us -> 859 us
    psum x1 -> x2, waiting for transfers between devices: 257 us -> 211 us  [per_device(): gram_matrix = lax.psum(lax.psum(gram_local, 'rows'), 'cols') / total_rows]
  transfers between devices with their start and end apart: 3 -> 4, of which waited for: 3 -> 4; matrix products, arithmetic and copies ran while one was open for 0% -> 0% of each run, Pallas kernels for 0% -> 0%
where the time goes in v1:
time: 1080 us
  waiting for transfers between devices  859 us (80%)
  local copies, waits for them, and re-layouts  99.9 us (9%)
  other arithmetic  61.6 us (6%)
  blocking collectives  20 us (2%)
  matrix products  17.3 us (2%)
  between operations  15.3 us (1%)
    all_to_all x1, waiting for transfers between devices, send_back(): lax.all_to_all(blocks, 'rows', split_axis=0, concat_axis=0, tiled=True)  577 us
    psum x2, waiting for transfers between devices, per_device(): gram_matrix = lax.psum(lax.psum(gram_local, 'rows'), 'cols') / total_rows  211 us
    reduce_scatter x1, waiting for transfers between devices, per_device(): lax.psum_scatter(partial_image, 'cols', scatter_dimension=0, tiled=True)  71.1 us
    gather x8, local copies, waits for them, and re-layouts, one_row(): picked = table[positions_row]  70.7 us
    another operation x6, other arithmetic, per_device(): lower_factor = jnp.linalg.cholesky(gram_matrix)  34 us
  transfers between devices with their start and end apart: 4, of which 4 were waited for; matrix products, arithmetic and copies ran while one was open for 0% of the time, Pallas kernels for 0%

profile of v1, /device:TPU:2, one launch (start us, length us, event | category | flops | bytes accessed | tf_op | source)
XLA Modules:
  0.0 1080.9 jit_solution(16640914202995419778)
XLA Ops:
  7.2 0.9 reshape.225
  8.1 0.8 reshape.224
  8.9 0.8 reshape.228
  10.6 1.4 scatter_custom_fusion
  12.1 20.0 %all_to_all.17 = s32[32,1,12]{2,1,0:T(1,128)S(1)} all-to-all(s32[32,1,12]{2,1,0:T(1,128)S(1)} %bitcast.99), channel_id=1, replica_groups=mesh['rows'=32,'cols'=8] {'rows'}, dimensions={0} | all-to-all | bytes 3072 | tf_op jit(solution)/shard_map/all_to_all | solution.py:49
  32.2 12.9 %gather_fusion.1 = bf16[384,128,256]{2,1,0:T(8,128)(2,1)} fusion(bf16[32,128,256]{2,1,0:T(8,128)(2,1)S(1)} %bitcast.94, s32[1024]{0:T(1024)S(1)} %pad_clamp_fusion.1), kind=kCustom, calls=%fused_computation.1 | custom fusion | bytes 50333184 | tf_op jit(solution)/shard_map/gather | solution.py:20
  45.1 6.5 all-to-all-start.1
  51.7 577.4 %all-to-all-done.1 = bf16[32,12,128,256]{3,2,1,0:T(8,128)(2,1)} async-done(((bf16[32,12,128,256]{3,2,1,0:T(8,128)(2,1)}), bf16[32,12,128,256]{3,2,1,0:T(8,128)(2,1)}, u32[]{:S(2)}, u32[]{:S(2)}) %all-to-all-start.1) | async-done | bytes 25165856 | tf_op jit(solution)/shard_map/all_to_all | solution.py:21
  629.1 95.0 %while.13 = (s32[]{:T(128)}, f32[8,128,256]{2,1,0:T(8,128)S(1)}, bf16[8,32,128,128]{3,2,1,0:T(8,128)(2,1)}, s32[8,32]{1,0:T(8,128)S(1)}, bf16[384,128,256]{2,1,0:T(8,128)(2,1)}, /*index=5*/s32[8,1]{0,1:T(1,128)S(1)}, s32[]{:T(128)}) while((s32[]{:T(128)}, f32[8,128,256]{2,1,0:T(8,128)S(1)}, bf16[8,32,128,128]{3,2,1,0:T(8,128)(2,1)}, ...), condition=%wide.region_5.6_spmd.clone, body=%wide.region_4.5_spmd.clone.sunk | while | flops 269485216 | bytes 7477409 | solution.py:35
  629.1 8.8 gather_fusion
  638.6 0.6 compare_convert_fusion.2
  639.2 1.8 fusion.53
  641.0 8.8 gather_fusion
  650.4 0.6 compare_convert_fusion.2
  651.1 1.8 fusion.53
  652.9 8.8 gather_fusion
  662.3 0.6 compare_convert_fusion.2
  663.0 1.8 fusion.53
  664.8 8.8 gather_fusion
  674.2 0.6 compare_convert_fusion.2
  674.8 1.8 fusion.53
  676.6 8.8 gather_fusion
  686.7 1.8 fusion.53
  688.5 8.8 gather_fusion
  698.6 1.8 fusion.53
  700.4 8.8 gather_fusion
  709.9 0.6 compare_convert_fusion.2
  710.5 1.8 fusion.53
  712.3 8.8 gather_fusion
  721.7 0.6 compare_convert_fusion.2
  722.4 1.8 fusion.53
  724.1 1.3 copy.23
  725.5 71.1 %reduce-scatter.2.cloned.1.call-done = f32[128,256]{0,1:T(8,128)} async-done(((f32[1024,256]{0,1:T(8,128)}), f32[128,256]{0,1:T(8,128)}) %reduce-scatter.2.cloned.1.call-update) | async-done | bytes 131088 | tf_op jit(solution)/shard_map/reduce_scatter | solution.py:54
  796.6 2.1 fusion.37
  798.9 144.9 %all-reduce.4.cloned.1.call-done = f32[256,256]{0,1:T(8,128)} async-done(((f32[256,256]{0,1:T(8,128)}), f32[256,256]{0,1:T(8,128)}) %all-reduce.4.cloned.1.call-update) | async-done | bytes 262160 | tf_op jit(solution)/shard_map/psum | solution.py:62
  943.9 66.0 %all-reduce.6.cloned.1.call-done = f32[256,256]{0,1:T(8,128)} async-done(((f32[256,256]{0,1:T(8,128)}), f32[256,256]{0,1:T(8,128)}) %all-reduce.6.cloned.1.call-update) | async-done | bytes 262160 | tf_op jit(solution)/shard_map/psum | solution.py:62
  1009.9 1.0 broadcast_multiply_fusion
  1011.0 1.0 fusion.16
  1012.0 11.7 %cholesky.50 = f32[128,128]{1,0:T(8,128)S(1)} custom-call(f32[128,128]{1,0:T(8,128)S(1)} %cholesky.118), custom_call_target="Cholesky" | custom-call | tf_op jit(solution)/shard_map/jit(cholesky)/cholesky | solution.py:63
  1023.8 9.8 custom-call.15
  1034.1 11.7 %cholesky.105 = f32[128,128]{1,0:T(8,128)S(1)} custom-call(f32[128,128]{1,0:T(8,128)S(1)} %convolution_subtract_fusion.1), custom_call_target="Cholesky" | custom-call | tf_op jit(solution)/shard_map/jit(cholesky)/cholesky | solution.py:63
  1045.8 0.7 compare_reduce_fusion
  1048.0 4.3 while.12
  1048.8 1.4 bitcast_dynamic-update-slice_fusion.2
  1050.9 1.4 bitcast_dynamic-update-slice_fusion.2
  1052.3 19.7 %custom-call.16 = f32[2,128,128]{1,2,0:T(8,128)S(1)} custom-call(f32[2,128,128]{2,1,0:T(8,128)S(1)} %get-tuple-element.47), custom_call_target="InvertDiagBlocksLowerTriangular" | custom-call | tf_op jit(solution)/shard_map/jit(_solve_triangular)/triangular_solve | solution.py:64
  1072.8 0.8 copy.20
  1073.6 0.8 copy.21
  (77 shorter events, 10.6 us)
Async XLA Ops:
  7.2 25.0 %copy-start = (bf16[4096,256]{1,0:T(8,128)(2,1)S(1)}, bf16[4096,256]{1,0:T(8,128)(2,1)}, u32[]{:S(2)}) copy-start(bf16[4096,256]{1,0:T(8,128)(2,1)} %param.9) | copy-start | bytes 6291460
  45.1 6.6 copy-start.3
  45.1 584.0 %copy-start.4 = (s32[8,1]{0,1:T(1,128)S(1)}, s32[8,1]{0,1:T(1,128)}, u32[]{:S(2)}) copy-start(s32[8,1]{0,1:T(1,128)} %param.8) | copy-start | bytes 100
  45.1 584.0 %all-to-all-start.1 = ((bf16[32,12,128,256]{3,2,1,0:T(8,128)(2,1)}), bf16[32,12,128,256]{3,2,1,0:T(8,128)(2,1)}, u32[]{:S(2)}, u32[]{:S(2)}) async-start(bf16[32,12,128,256]{3,2,1,0:T(8,128)(2,1)} %bitcast.95), calls=%async_computation.1 | async-start | bytes 50331648 | tf_op jit(solution)/shard_map/all_to_all | solution.py:21
  51.6 745.0 %reduce-scatter.2.cloned.1.call-start = ((), (), s32[]{:S(2)}) async-start(), calls=%async_computation.3 | async-start | bytes 1179648 | tf_op jit(solution)/shard_map/reduce_scatter | solution.py:54
  725.5 218.3 %all-reduce.4.cloned.1.call-start = ((), (), s32[]{:S(2)}) async-start(), calls=%async_computation.4 | async-start | bytes 524288 | tf_op jit(solution)/shard_map/psum | solution.py:62
  798.7 211.2 %all-reduce.6.cloned.1.call-start = ((), (), s32[]{:S(2)}) async-start(), calls=%async_computation.5 | async-start | bytes 524288 | tf_op jit(solution)/shard_map/psum | solution.py:62
  1010.9 61.1 %copy-start.2 = (f32[128,256]{0,1:T(8,128)S(1)}, f32[128,256]{0,1:T(8,128)}, u32[]{:S(2)}) copy-start(f32[128,256]{0,1:T(8,128)} %reduce-scatter.2.cloned.1.call-done) | copy-start | bytes 393220
  1023.8 50.6 %copy-start.1 = (bf16[4096,256]{1,0:T(8,128)(2,1)S(1)}, bf16[4096,256]{1,0:T(8,128)(2,1)}, u32[]{:S(2)}) copy-start(bf16[4096,256]{1,0:T(8,128)(2,1)} %param.9) | copy-start | bytes 6291460
Sparse Core Ops, SparseCore 0:
  725.6 70.9 reduce-scatter.1
  800.6 143.1 all-reduce.3
  946.2 63.6 all-reduce.5
